TPU v7x, 256 devices: a whole 4x4x8 slice. The times are simulated.
256 devices in a mesh: req: 32 (over x, y, core), exp: 8 (over z).
Axes of the slice: x: 4, y: 4, z: 8, core: 2. Of those that a mesh axis runs over, the one named last changes fastest.
Arguments:
- residual: bfloat16 [4096, 2048], P(('req', 'exp')), may hold values from -12 to 12
- queries: bfloat16 [4096, 2, 2048], P('req', None, 'exp'), may hold values from -9 to 9
- kv_cache: bfloat16 [608, 2, 128, 2048], P('req', None, None, 'exp'), may hold values from -4 to 4
- page_table: int32 [288, 11], P('req'), may hold values from 0 to 18, as said below
- seq_lengths: int32 [288], P('req'), may hold values from 8 to 1408, as said below
- head_route: int32 [4096, 2], P('req'), may hold values from 0 to 7, all different within a row
- head_gate: float32 [4096, 2], P('req'), may hold values from 0.2 to 1
- out_weight: bfloat16 [8, 2048, 2048], P(None, 'exp'), may hold values from -0.5 to 0.5
- norm_gain: float32 [2048], replicated, may hold values from 0.25 to 1.75
- expert_route: int32 [4096, 2], P(('req', 'exp')), may hold values from 0 to 7, all different within a row; in each aligned block of 16 rows (0 to 15, 16 to 31, ...) at most 8 rows name the same one
- expert_gate: float32 [4096, 2], P(('req', 'exp')), may hold values from 0.2 to 1
- gate_up: bfloat16 [8, 2, 2048, 5632], P('exp', None, None, 'req'), may hold values from -0.125 to 0.125
- down_weight: bfloat16 [8, 5632, 2048], P('exp', 'req'), may hold values from -0.078125 to 0.078125
Outputs:
- attended: bfloat16 [4096, 2048], P(('req', 'exp'))
- expert_mix: bfloat16 [4096, 2048], P(('req', 'exp'))
Inputs may be any that keep to these rules, and one draw needn't show every extreme that they name: `page_table`: pages are numbered within the slot's group. A group's slot 0 lists 11 different pages; each other slot repeats one page along its row; no two slots of a group share a page. `seq_lengths`: slot 0 of every group is a prefill request of length at least 120; the other slots are decode requests of length at most 128. `head_route`: each row names 2 different attention experts. `expert_route`: each row names 2 different experts; within the rows of one device no expert is named by more than 8 rows.
All inputs are finite; a program needn't handle non-finite values.
Results may differ from a plain program's by a relative error of at most 0.023.
Values may be sent and summed in bfloat16 or wider, within the bound.
A program may use at most 128 MiB of HBM per device.

v0:
```python
import jax
import jax.numpy as jnp
from jax import lax
from jax.sharding import PartitionSpec as P

HD = 128
TOPA = 2
SPAN = 120


def attend_local(queries_one, key_rows, value_rows, positions, head_count):
    amount = queries_one.shape[0]
    heads_q = queries_one.reshape(amount * TOPA, head_count, HD)
    heads_k = key_rows.reshape(-1, head_count, HD)
    heads_v = value_rows.reshape(-1, head_count, HD)
    scores = jnp.einsum(
        "qhd,khd->hqk", heads_q, heads_k, preferred_element_type=jnp.float32
    ) * HD ** (-0.5)
    key_pos = jnp.arange(heads_k.shape[0], dtype=jnp.int32)
    row_pos = jnp.repeat(positions, TOPA)
    allowed = key_pos[None, :] <= row_pos[:, None]
    scores = jnp.where(allowed[None], scores, -1e30)
    row_max = jnp.max(scores, axis=2, keepdims=True)
    raised = jnp.exp(scores - row_max)
    attention_weights = (raised / jnp.sum(raised, axis=2, keepdims=True)).astype(jnp.bfloat16)
    mixture = jnp.einsum(
        "hqk,khd->qhd", attention_weights, heads_v, preferred_element_type=jnp.float32
    )
    return mixture.astype(jnp.bfloat16).reshape(amount, TOPA, head_count * HD)


def local(
    residual,
    queries,
    kv_cache,
    page_table,
    seq_lengths,
    head_route,
    head_gate,
    out_weight,
    norm_gain,
    expert_route,
    expert_gate,
    gate_up,
    down_weight,
):
    feature_width = queries.shape[2]
    head_count = feature_width // HD
    page_rows = kv_cache[page_table[0]]
    key_rows = page_rows[:, 0].reshape(-1, feature_width)
    value_rows = page_rows[:, 1].reshape(-1, feature_width)
    prefill_pos = seq_lengths[0] - SPAN + jnp.arange(SPAN, dtype=jnp.int32)
    prefill_out = attend_local(queries[:SPAN], key_rows, value_rows, prefill_pos, head_count)
    decode_pages = kv_cache[page_table[1:, 0]]

    def decode_one(query_row, page_block, length):
        return attend_local(
            query_row[None], page_block[0], page_block[1], (length - 1)[None], head_count
        )[0]

    decode_out = jax.vmap(decode_one)(queries[SPAN:], decode_pages, seq_lengths[1:])
    mixture = jnp.concatenate([prefill_out, decode_out], axis=0)
    partial_value = jnp.zeros((mixture.shape[0], residual.shape[1]), jnp.float32)
    for expert_index in range(out_weight.shape[0]):
        picked = head_route == expert_index
        chosen = jnp.sum(jnp.where(picked[:, :, None], mixture, jnp.zeros_like(mixture)), axis=1)
        weight = jnp.sum(jnp.where(picked, head_gate, jnp.zeros_like(head_gate)), axis=1)
        partial_value = partial_value + weight[:, None] * jnp.dot(
            chosen, out_weight[expert_index], preferred_element_type=jnp.float32
        )
    row_count = residual.shape[0]
    summed = lax.psum(partial_value.astype(jnp.bfloat16), "exp").astype(jnp.float32)
    own_heads = lax.dynamic_slice_in_dim(summed, lax.axis_index("exp") * row_count, row_count, 0)
    attended = (residual.astype(jnp.float32) + own_heads).astype(jnp.bfloat16)
    values_f = attended.astype(jnp.float32)
    normed = (
        values_f
        * lax.rsqrt(jnp.mean(values_f * values_f, axis=1, keepdims=True) + 1e-06)
        * norm_gain
    ).astype(jnp.bfloat16)
    experts = lax.axis_size("exp")
    capacity = max(2, 2 * TOPA * row_count // experts)
    flat_route = expert_route.reshape(-1)
    onehot = (flat_route[:, None] == jnp.arange(experts, dtype=jnp.int32)[None, :]).astype(
        jnp.int32
    )
    earlier = jnp.cumsum(onehot, axis=0) - onehot
    rank_index = jnp.sum(earlier * onehot, axis=1)
    slot_index = flat_route * capacity + rank_index
    placing = (
        jnp.arange(experts * capacity, dtype=jnp.int32)[:, None] == slot_index[None, :]
    ).astype(jnp.bfloat16)
    repeated = jnp.repeat(normed, TOPA, axis=0)
    outgoing = jnp.dot(placing, repeated, preferred_element_type=jnp.float32).astype(jnp.bfloat16)
    w_gate = gate_up[0, 0]
    w_up = gate_up[0, 1]
    w_down = down_weight[0]
    arrived = lax.all_to_all(outgoing, "exp", split_axis=0, concat_axis=0, tiled=True)
    portion = lax.all_gather(arrived, "req", axis=0, tiled=True)
    gate_part = jnp.dot(portion, w_gate, preferred_element_type=jnp.float32)
    up_part = jnp.dot(portion, w_up, preferred_element_type=jnp.float32)
    active = (jax.nn.silu(gate_part) * up_part).astype(jnp.bfloat16)
    portion = active
    returned = lax.psum_scatter(
        jnp.dot(portion, w_down, preferred_element_type=jnp.float32).astype(jnp.bfloat16),
        "req",
        scatter_dimension=0,
        tiled=True,
    )
    homeward = lax.all_to_all(returned, "exp", split_axis=0, concat_axis=0, tiled=True)
    picked_rows = jnp.take(homeward, slot_index, axis=0).astype(jnp.float32)
    weighted = picked_rows * expert_gate.reshape(-1)[:, None]
    expert_mix = jnp.sum(weighted.reshape(row_count, TOPA, -1), axis=1).astype(jnp.bfloat16)
    return (attended, expert_mix)


def solution(mesh):
    return jax.shard_map(
        local,
        mesh=mesh,
        in_specs=(
            P(("req", "exp"), None),
            P("req", None, "exp"),
            P("req", None, None, "exp"),
            P("req", None),
            P("req"),
            P("req", None),
            P("req", None),
            P(None, "exp", None),
            P(),
            P(("req", "exp"), None),
            P(("req", "exp"), None),
            P("exp", None, None, "req"),
            P("exp", "req", None),
        ),
        out_specs=(P(("req", "exp"), None), P(("req", "exp"), None)),
        check_vma=False,
    )
```

profile of v0, /device:TPU:2, one launch (start us, length us, event | category | flops | bytes accessed | tf_op | source)
XLA Modules:
  0.0 351.9 jit_solution(16315062266536121598)
XLA Ops:
  8.9 1.3 select_reduce_fusion.1
  15.4 1.8 gather_fusion
  17.2 2.4 fusion.83
  19.6 2.6 reshape_reshape_squeeze.7
  25.2 3.9 %fusion.86 = (f32[2,240]{1,0:T(2,128)S(1)}, f32[2,240,1408]{2,1,0:T(8,128)}) fusion(pred[240,1408]{1,0:T(8,128)(4,1)} %iota_compare_fusion, bf16[1408,2,128]{2,1,0:T(2,128)(2,1)} %reshape_reshape_squeeze.7, bf16[240,2,128]{2,1,0:T(2,128)(2,1)S(1)} %reshape.164), kind=kOutput, calls=%fused_computation.145 | convolution fusion | flops 175719808 | bytes 3886976 | tf_op jit(solution)/shard_map/sub | solution.py:24
  29.0 2.4 fusion.18
  38.5 2.2 fusion.85
  41.9 3.8 %fusion.63 = (bf16[128,256]{1,0:T(8,128)(2,1)S(1)}, bf16[128,256]{1,0:T(8,128)(2,1)S(1)}, bf16[128,256]{1,0:T(8,128)(2,1)S(1)}, bf16[128,256]{1,0:T(8,128)(2,1)S...) fusion(pred[128,2]{1,0:T(8,128)(4,1)} %copy.77, ...), kind=kLoop, calls=%fused_computation.90 | loop fusion | flops 851968 | bytes 657408 | tf_op jit(solution)/shard_map/reduce_sum | solution.py:66
  45.7 1.5 convolution_multiply_fusion.9
  47.3 1.5 fusion.13
  48.9 1.5 fusion.12
  50.4 1.5 fusion.11
  52.0 1.5 fusion.10
  53.6 1.5 fusion.9
  55.2 1.6 fusion.8
  56.7 2.4 fusion.14
  59.7 76.3 %all-reduce.2.cloned.1.call-done = bf16[128,2048]{1,0:T(8,128)(2,1)} async-done(((bf16[128,2048]{1,0:T(8,128)(2,1)}), bf16[128,2048]{1,0:T(8,128)(2,1)}) %all-reduce.2.cloned.1.call-update) | async-done | bytes 524304 | tf_op jit(solution)/shard_map/psum | solution.py:72
  137.4 14.4 %all_to_all.24 = bf16[8,8,2048]{2,1,0:T(8,128)(2,1)} all-to-all(bf16[8,8,2048]{2,1,0:T(8,128)(2,1)S(1)} %fusion.15), channel_id=1, replica_groups=mesh['req'=32,'exp'=8] {'exp'}, dimensions={0} | all-to-all | bytes 524288 | tf_op jit(solution)/shard_map/all_to_all | solution.py:98
  152.1 53.8 %all-gather.2.cloned.1.call-done = bf16[2048,2048]{1,0:T(8,128)(2,1)} async-done(((bf16[64,2048]{1,0:T(8,128)(2,1)}), bf16[2048,2048]{1,0:T(8,128)(2,1)}) %all-gather.2.cloned.1.call-update) | async-done | bytes 8388624 | tf_op jit(solution)/shard_map/all_gather | solution.py:99
  205.9 7.5 %fusion.43 = f32[2048,176]{0,1:T(8,128)} fusion(bf16[2048,2048]{1,0:T(8,128)(2,1)} %all-gather.2.cloned.1.call-done, bf16[1,2,2048,176]{2,3,1,0:T(8,128)(2,1)} %param.24), kind=kOutput, calls=%fused_computation.61 | convolution fusion | flops 1476395008 | bytes 10551296 | tf_op jit(solution)/shard_map/dot_general | solution.py:100
  213.5 12.5 %convolution_convert_fusion = bf16[2048,2048]{1,0:T(8,128)(2,1)} fusion(bf16[2048,2048]{1,0:T(8,128)(2,1)} %all-gather.2.cloned.1.call-done, f32[2048,176]{0,1:T(8,128)} %fusion.43, bf16[1,176,2048]{2,1,0:T(8,128)(2,1)} %param.25, bf16[1,2,2048,176]{2,3,1,0:T(8,128)(2,1)} %param.24), kind=kOutput, calls=%fused_computation.5 | convolution fusion | flops 2959147008 | bytes 19660800 | tf_op jit(solution)/shard_map/dot_general | solution.py:105
  226.4 99.6 %reduce-scatter.2.cloned.1.call-done = bf16[64,2048]{1,0:T(8,128)(2,1)} async-done(((bf16[2048,2048]{1,0:T(8,128)(2,1)}), bf16[64,2048]{1,0:T(8,128)(2,1)}) %reduce-scatter.2.cloned.1.call-update) | async-done | bytes 262160 | tf_op jit(solution)/shard_map/reduce_scatter | solution.py:104
  326.0 7.0 %all-to-all-start.1 = ((bf16[8,8,2048]{2,1,0:T(8,128)(2,1)}), bf16[8,8,2048]{2,1,0:T(8,128)(2,1)S(1)}, u32[]{:S(2)}, u32[]{:S(2)}) async-start(bf16[8,8,2048]{2,1,0:T(8,128)(2,1)} %bitcast.101), calls=%async_computation.2 | async-start | bytes 524288 | tf_op jit(solution)/shard_map/all_to_all | solution.py:110
  333.2 10.3 %all-to-all-done.1 = bf16[8,8,2048]{2,1,0:T(8,128)(2,1)S(1)} async-done(((bf16[8,8,2048]{2,1,0:T(8,128)(2,1)}), bf16[8,8,2048]{2,1,0:T(8,128)(2,1)S(1)}, u32[]{:S(2)}, u32[]{:S(2)}) %all-to-all-start.1) | async-done | bytes 262176 | tf_op jit(solution)/shard_map/all_to_all | solution.py:110
  (90 shorter events, 22.8 us)
Async XLA Ops:
  7.2 8.2 %copy-start = (bf16[19,2,128,256]{3,2,1,0:T(8,128)(2,1)S(1)}, bf16[19,2,128,256]{3,2,1,0:T(8,128)(2,1)}, u32[]{:S(2)}) copy-start(bf16[19,2,128,256]{3,2,1,0:T(8,128)(2,1)} %param.15) | copy-start | bytes 7471108
  7.2 128.8 %all-reduce.2.cloned.1.call-start = ((), (), s32[]{:S(2)}) async-start(), calls=%async_computation.3 | async-start | bytes 1048576 | tf_op jit(solution)/shard_map/psum | solution.py:72
  17.2 5.0 %copy-start.14 = (s32[9]{0:T(128)S(1)}, s32[9]{0:T(128)}, u32[]{:S(2)}) copy-start(s32[9]{0:T(128)} %param.17) | copy-start | bytes 112
  17.2 6.8 %slice-start = ((bf16[128,2,256]{2,1,0:T(2,128)(2,1)}), bf16[120,2,256]{2,1,0:T(2,128)(2,1)S(1)}, s32[]{:S(2)}) async-start(bf16[128,2,256]{2,1,0:T(2,128)(2,1)} %param.14), calls=%async_computation.6 | async-start | bytes 245760 | tf_op jit(solution)/shard_map/slice | solution.py:53
  25.2 3.9 %copy-start.1 = (bf16[1408,2,128]{2,1,0:T(2,128)(2,1)S(1)}, bf16[1408,2,128]{2,1,0:T(2,128)(2,1)}, u32[]{:S(2)}) copy-start(bf16[1408,2,128]{2,1,0:T(2,128)(2,1)} %reshape_reshape_squeeze.6) | copy-start | bytes 2162692
  40.8 6.5 %copy-start.12 = (f32[128]{0:T(128)S(1)}, f32[128]{0:T(128)}, u32[]{:S(2)}) copy-start(f32[128]{0:T(128)} %get-tuple-element.15) | copy-start | bytes 1540
  45.7 3.1 copy-start.11
  47.3 3.1 copy-start.10
  48.9 3.1 copy-start.9
  50.4 3.1 copy-start.8
  52.0 3.1 copy-start.7
  53.6 3.2 copy-start.6
  55.1 4.1 %copy-start.4 = (s32[16,2]{0,1:T(2,128)S(1)}, s32[16,2]{0,1:T(2,128)}, u32[]{:S(2)}) copy-start(s32[16,2]{0,1:T(2,128)} %param.22) | copy-start | bytes 388
  55.1 80.8 %copy-start.3 = (bf16[16,2048]{1,0:T(8,128)(2,1)S(1)}, bf16[16,2048]{1,0:T(8,128)(2,1)}, u32[]{:S(2)}) copy-start(bf16[16,2048]{1,0:T(8,128)(2,1)} %param.13) | copy-start | bytes 196612
  55.1 81.8 %copy-start.5 = (f32[2048]{0:T(1024)S(1)}, f32[2048]{0:T(1024)}, u32[]{:S(2)}) copy-start(f32[2048]{0:T(1024)} %param.21) | copy-start | bytes 24580
  59.1 146.8 %all-gather.2.cloned.1.call-start = ((), (), s32[]{:S(2)}) async-start(), calls=%async_computation.4 | async-start | bytes 8650752 | tf_op jit(solution)/shard_map/all_gather | solution.py:99
  137.0 76.5 %copy-start.2 = (bf16[16,2048]{1,0:T(8,128)(2,1)}, bf16[16,2048]{1,0:T(8,128)(2,1)S(1)}, u32[]{:S(2)}) copy-start(bf16[16,2048]{1,0:T(8,128)(2,1)S(1)} %get-tuple-element.19) | copy-start | bytes 196612
  151.9 174.1 %reduce-scatter.2.cloned.1.call-start = ((), (), s32[]{:S(2)}) async-start(), calls=%async_computation.5 | async-start | bytes 8650752 | tf_op jit(solution)/shard_map/reduce_scatter | solution.py:104
  226.0 107.1 %copy-start.13 = (f32[16,2]{0,1:T(2,128)S(1)}, f32[16,2]{0,1:T(2,128)}, u32[]{:S(2)}) copy-start(f32[16,2]{0,1:T(2,128)} %param.23) | copy-start | bytes 388
  326.0 17.5 %all-to-all-start.1 = ((bf16[8,8,2048]{2,1,0:T(8,128)(2,1)}), bf16[8,8,2048]{2,1,0:T(8,128)(2,1)S(1)}, u32[]{:S(2)}, u32[]{:S(2)}) async-start(bf16[8,8,2048]{2,1,0:T(8,128)(2,1)} %bitcast.101), calls=%async_computation.2 | async-start | bytes 524288 | tf_op jit(solution)/shard_map/all_to_all | solution.py:110
Sparse Core Ops, SparseCore 0:
  59.2 76.6 all-reduce.1
  152.0 53.8 all-gather.1
  226.2 99.7 reduce-scatter.1
where the time goes:
time: 353 us; the launch traced here: 352 us
  waiting for transfers between devices  240 us (68%)
  matrix products  43 us (12%)
  local copies, waits for them, and re-layouts  20.2 us (6%)
  blocking collectives  14.4 us (4%)
  between operations  14.1 us (4%)
  other arithmetic  12.8 us (4%)
  starting transfers between devices  7.29 us (2%)
    reduce_scatter x1, waiting for transfers between devices, local(): lax.psum_scatter(jnp.dot(portion, w_down, preferred_element_type=jnp.floa...  99.6 us
    psum x1, waiting for transfers between devices, local(): lax.psum(partial_value.astype(jnp.bfloat16), 'exp').astype(jnp.float32)  76.3 us
    all_gather x1, waiting for transfers between devices, local(): portion = lax.all_gather(arrived, 'req', axis=0, tiled=True)  53.8 us
    all_to_all x1, blocking collectives, local(): lax.all_to_all(outgoing, 'exp', split_axis=0, concat_axis=0, tiled=True)  14.4 us
    dot_general x8, matrix products, local(): jnp.dot(chosen, out_weight[expert_index], preferred_element_type=jnp.floa...  13.1 us
    dot_general x1, matrix products, local(): jnp.dot(portion, w_down, preferred_element_type=jnp.float32)  12.5 us
    all_to_all x1, waiting for transfers between devices, local(): lax.all_to_all(returned, 'exp', split_axis=0, concat_axis=0, tiled=True)  10.3 us
    dot_general x1, matrix products, local(): gate_part = jnp.dot(portion, w_gate, preferred_element_type=jnp.float32)  7.55 us
  transfers between devices with their start and end apart: 4, of which 4 were waited for; matrix products, arithmetic and copies ran while one was open for 0% of the time, Pallas kernels for 0%

commit v1 on v0

--- a/solution.py
+++ b/solution.py
@@ -69,7 +69,9 @@
             chosen, out_weight[expert_index], preferred_element_type=jnp.float32
         )
     row_count = residual.shape[0]
-    summed = lax.psum(partial_value.astype(jnp.bfloat16), "exp").astype(jnp.float32)
+    summed = jnp.sum(lax.all_gather(partial_value.astype(jnp.bfloat16), "exp"), axis=0).astype(
+        jnp.float32
+    )
     own_heads = lax.dynamic_slice_in_dim(summed, lax.axis_index("exp") * row_count, row_count, 0)
     attended = (residual.astype(jnp.float32) + own_heads).astype(jnp.bfloat16)
     values_f = attended.astype(jnp.float32)

time: 353 us -> 338 us (0.958)
  waiting for transfers between devices: 240 us -> 221 us
    psum x1 -> x0, waiting for transfers between devices: 76.3 us -> none  [local(): lax.psum(partial_value.astype(jnp.bfloat16), 'exp').astype(jnp.float32)]
    all_gather x0 -> x1, waiting for transfers between devices: none -> 57.3 us  [local(): lax.all_gather(partial_value.astype(jnp.bfloat16), 'exp')]
where the time goes in v1:
time: 338 us; the launch traced here: 337 us
  waiting for transfers between devices  221 us (65%)
  matrix products  43 us (13%)
  local copies, waits for them, and re-layouts  20.2 us (6%)
  blocking collectives  15.9 us (5%)
  other arithmetic  15 us (4%)
  between operations  14.1 us (4%)
  starting transfers between devices  7.35 us (2%)
    reduce_scatter x1, waiting for transfers between devices, local(): lax.psum_scatter(jnp.dot(portion, w_down, preferred_element_type=jnp.floa...  99.6 us
    all_gather x1, waiting for transfers between devices, local(): lax.all_gather(partial_value.astype(jnp.bfloat16), 'exp')  57.3 us
    all_gather x1, waiting for transfers between devices, local(): portion = lax.all_gather(arrived, 'req', axis=0, tiled=True)  53.8 us
    all_to_all x1, blocking collectives, local(): lax.all_to_all(outgoing, 'exp', split_axis=0, concat_axis=0, tiled=True)  15.9 us
    dot_general x8, matrix products, local(): jnp.dot(chosen, out_weight[expert_index], preferred_element_type=jnp.floa...  13.1 us
    dot_general x1, matrix products, local(): jnp.dot(portion, w_down, preferred_element_type=jnp.float32)  12.5 us
    all_to_all x1, waiting for transfers between devices, local(): lax.all_to_all(returned, 'exp', split_axis=0, concat_axis=0, tiled=True)  10.3 us
    dot_general x1, matrix products, local(): gate_part = jnp.dot(portion, w_gate, preferred_element_type=jnp.float32)  7.55 us
  transfers between devices with their start and end apart: 4, of which 4 were waited for; matrix products, arithmetic and copies ran while one was open for 0% of the time, Pallas kernels for 0%

profile of v1, /device:TPU:2, one launch (start us, length us, event | category | flops | bytes accessed | tf_op | source)
XLA Modules:
  0.0 336.5 jit_solution(1039703793063086567)
XLA Ops:
  15.4 1.8 gather_fusion
  17.2 2.4 fusion.83
  19.6 2.6 reshape_reshape_squeeze.7
  25.2 3.9 %fusion.86 = (f32[2,240]{1,0:T(2,128)S(1)}, f32[2,240,1408]{2,1,0:T(8,128)}) fusion(pred[240,1408]{1,0:T(8,128)(4,1)} %iota_compare_fusion, bf16[1408,2,128]{2,1,0:T(2,128)(2,1)} %reshape_reshape_squeeze.7, bf16[240,2,128]{2,1,0:T(2,128)(2,1)S(1)} %reshape.164), kind=kOutput, calls=%fused_computation.145 | convolution fusion | flops 175719808 | bytes 3886976 | tf_op jit(solution)/shard_map/sub | solution.py:24
  29.0 2.4 fusion.18
  38.5 2.2 fusion.85
  41.9 3.8 %fusion.63 = (bf16[128,256]{1,0:T(8,128)(2,1)S(1)}, bf16[128,256]{1,0:T(8,128)(2,1)S(1)}, bf16[128,256]{1,0:T(8,128)(2,1)S(1)}, bf16[128,256]{1,0:T(8,128)(2,1)S...) fusion(pred[128,2]{1,0:T(8,128)(4,1)} %copy.77, ...), kind=kLoop, calls=%fused_computation.90 | loop fusion | flops 851968 | bytes 657408 | tf_op jit(solution)/shard_map/reduce_sum | solution.py:66
  45.7 1.5 convolution_multiply_fusion.9
  47.3 1.5 fusion.13
  48.9 1.5 fusion.12
  50.4 1.5 fusion.11
  52.0 1.5 fusion.10
  53.6 1.5 fusion.9
  55.1 1.5 fusion.8
  56.7 2.3 fusion.14
  59.6 57.3 %all-gather.6.cloned.1.call-done = bf16[1024,2048]{1,0:T(8,128)(2,1)} async-done(((bf16[128,2048]{1,0:T(8,128)(2,1)}), bf16[1024,2048]{1,0:T(8,128)(2,1)}) %all-gather.6.cloned.1.call-update) | async-done | bytes 4194320 | tf_op jit(solution)/shard_map/all_gather | solution.py:72
  116.9 3.0 reduce_sum.247
  120.5 15.9 %all_to_all.24 = bf16[8,8,2048]{2,1,0:T(8,128)(2,1)} all-to-all(bf16[8,8,2048]{2,1,0:T(8,128)(2,1)S(1)} %fusion.15), channel_id=1, replica_groups=mesh['req'=32,'exp'=8] {'exp'}, dimensions={0} | all-to-all | bytes 524288 | tf_op jit(solution)/shard_map/all_to_all | solution.py:100
  136.7 53.8 %all-gather.4.cloned.1.call-done = bf16[2048,2048]{1,0:T(8,128)(2,1)} async-done(((bf16[64,2048]{1,0:T(8,128)(2,1)}), bf16[2048,2048]{1,0:T(8,128)(2,1)}) %all-gather.4.cloned.1.call-update) | async-done | bytes 8388624 | tf_op jit(solution)/shard_map/all_gather | solution.py:101
  190.5 7.5 %fusion.43 = f32[2048,176]{0,1:T(8,128)} fusion(bf16[2048,2048]{1,0:T(8,128)(2,1)} %all-gather.4.cloned.1.call-done, bf16[1,2,2048,176]{2,3,1,0:T(8,128)(2,1)} %param.24), kind=kOutput, calls=%fused_computation.61 | convolution fusion | flops 1476395008 | bytes 10551296 | tf_op jit(solution)/shard_map/dot_general | solution.py:102
  198.1 12.5 %convolution_convert_fusion = bf16[2048,2048]{1,0:T(8,128)(2,1)} fusion(bf16[2048,2048]{1,0:T(8,128)(2,1)} %all-gather.4.cloned.1.call-done, f32[2048,176]{0,1:T(8,128)} %fusion.43, bf16[1,176,2048]{2,1,0:T(8,128)(2,1)} %param.25, bf16[1,2,2048,176]{2,3,1,0:T(8,128)(2,1)} %param.24), kind=kOutput, calls=%fused_computation.5 | convolution fusion | flops 2959147008 | bytes 19660800 | tf_op jit(solution)/shard_map/dot_general | solution.py:107
  211.0 99.6 %reduce-scatter.2.cloned.1.call-done = bf16[64,2048]{1,0:T(8,128)(2,1)} async-done(((bf16[2048,2048]{1,0:T(8,128)(2,1)}), bf16[64,2048]{1,0:T(8,128)(2,1)}) %reduce-scatter.2.cloned.1.call-update) | async-done | bytes 262160 | tf_op jit(solution)/shard_map/reduce_scatter | solution.py:106
  310.5 7.0 %all-to-all-start.1 = ((bf16[8,8,2048]{2,1,0:T(8,128)(2,1)}), bf16[8,8,2048]{2,1,0:T(8,128)(2,1)S(1)}, u32[]{:S(2)}, u32[]{:S(2)}) async-start(bf16[8,8,2048]{2,1,0:T(8,128)(2,1)} %bitcast.103), calls=%async_computation.2 | async-start | bytes 524288 | tf_op jit(solution)/shard_map/all_to_all | solution.py:112
  317.8 10.3 %all-to-all-done.1 = bf16[8,8,2048]{2,1,0:T(8,128)(2,1)S(1)} async-done(((bf16[8,8,2048]{2,1,0:T(8,128)(2,1)}), bf16[8,8,2048]{2,1,0:T(8,128)(2,1)S(1)}, u32[]{:S(2)}, u32[]{:S(2)}) %all-to-all-start.1) | async-done | bytes 262176 | tf_op jit(solution)/shard_map/all_to_all | solution.py:112
  (91 shorter events, 23.3 us)
Async XLA Ops:
  7.2 8.2 %copy-start = (bf16[19,2,128,256]{3,2,1,0:T(8,128)(2,1)S(1)}, bf16[19,2,128,256]{3,2,1,0:T(8,128)(2,1)}, u32[]{:S(2)}) copy-start(bf16[19,2,128,256]{3,2,1,0:T(8,128)(2,1)} %param.15) | copy-start | bytes 7471108
  7.2 109.7 %all-gather.6.cloned.1.call-start = ((), (), s32[]{:S(2)}) async-start(), calls=%async_computation.5 | async-start | bytes 4718592 | tf_op jit(solution)/shard_map/all_gather | solution.py:72
  17.2 5.0 %copy-start.14 = (s32[9]{0:T(128)S(1)}, s32[9]{0:T(128)}, u32[]{:S(2)}) copy-start(s32[9]{0:T(128)} %param.17) | copy-start | bytes 112
  17.2 6.8 %slice-start = ((bf16[128,2,256]{2,1,0:T(2,128)(2,1)}), bf16[120,2,256]{2,1,0:T(2,128)(2,1)S(1)}, s32[]{:S(2)}) async-start(bf16[128,2,256]{2,1,0:T(2,128)(2,1)} %param.14), calls=%async_computation.6 | async-start | bytes 245760 | tf_op jit(solution)/shard_map/slice | solution.py:53
  25.2 3.9 %copy-start.1 = (bf16[1408,2,128]{2,1,0:T(2,128)(2,1)S(1)}, bf16[1408,2,128]{2,1,0:T(2,128)(2,1)}, u32[]{:S(2)}) copy-start(bf16[1408,2,128]{2,1,0:T(2,128)(2,1)} %reshape_reshape_squeeze.6) | copy-start | bytes 2162692
  40.8 6.5 %copy-start.12 = (f32[128]{0:T(128)S(1)}, f32[128]{0:T(128)}, u32[]{:S(2)}) copy-start(f32[128]{0:T(128)} %get-tuple-element.15) | copy-start | bytes 1540
  45.7 3.1 copy-start.11
  47.3 3.1 copy-start.10
  48.9 3.1 copy-start.9
  50.4 3.1 copy-start.8
  52.0 3.1 copy-start.7
  53.6 3.1 copy-start.6
  55.1 4.0 %copy-start.4 = (s32[16,2]{0,1:T(2,128)S(1)}, s32[16,2]{0,1:T(2,128)}, u32[]{:S(2)}) copy-start(s32[16,2]{0,1:T(2,128)} %param.22) | copy-start | bytes 388
  59.0 60.8 %copy-start.3 = (bf16[16,2048]{1,0:T(8,128)(2,1)S(1)}, bf16[16,2048]{1,0:T(8,128)(2,1)}, u32[]{:S(2)}) copy-start(bf16[16,2048]{1,0:T(8,128)(2,1)} %param.13) | copy-start | bytes 196612
  59.0 61.0 %copy-start.5 = (f32[2048]{0:T(1024)S(1)}, f32[2048]{0:T(1024)}, u32[]{:S(2)}) copy-start(f32[2048]{0:T(1024)} %param.21) | copy-start | bytes 24580
  59.1 131.4 %all-gather.4.cloned.1.call-start = ((), (), s32[]{:S(2)}) async-start(), calls=%async_computation.3 | async-start | bytes 8650752 | tf_op jit(solution)/shard_map/all_gather | solution.py:101
  120.0 78.0 %copy-start.2 = (bf16[16,2048]{1,0:T(8,128)(2,1)}, bf16[16,2048]{1,0:T(8,128)(2,1)S(1)}, u32[]{:S(2)}) copy-start(bf16[16,2048]{1,0:T(8,128)(2,1)S(1)} %get-tuple-element.19) | copy-start | bytes 196612
  136.4 174.1 %reduce-scatter.2.cloned.1.call-start = ((), (), s32[]{:S(2)}) async-start(), calls=%async_computation.4 | async-start | bytes 8650752 | tf_op jit(solution)/shard_map/reduce_scatter | solution.py:106
  210.6 107.1 %copy-start.13 = (f32[16,2]{0,1:T(2,128)S(1)}, f32[16,2]{0,1:T(2,128)}, u32[]{:S(2)}) copy-start(f32[16,2]{0,1:T(2,128)} %param.23) | copy-start | bytes 388
  310.5 17.5 %all-to-all-start.1 = ((bf16[8,8,2048]{2,1,0:T(8,128)(2,1)}), bf16[8,8,2048]{2,1,0:T(8,128)(2,1)S(1)}, u32[]{:S(2)}, u32[]{:S(2)}) async-start(bf16[8,8,2048]{2,1,0:T(8,128)(2,1)} %bitcast.103), calls=%async_computation.2 | async-start | bytes 524288 | tf_op jit(solution)/shard_map/all_to_all | solution.py:112
Sparse Core Ops, SparseCore 0:
  59.2 57.6 all-gather.5
  136.6 53.8 all-gather.3
  210.7 99.7 reduce-scatter.1
